TPU v7x, 512 devices: a whole 4x8x8 slice. The times are simulated.
512 devices in a mesh: blk: 8 (over z_lo, core), owner: 64 (over z_hi, x, y).
Axes of the slice: x: 4, y: 8, z: 8 (z_hi: 2, z_lo: 4; z = z_hi * 4 + z_lo), core: 2. Of those that a mesh axis runs over, the one named last changes fastest.
Arguments:
- tokens: bfloat16 [2048, 32, 1024], P(('owner', 'blk')), may hold values from -6 to 6
- w_qkv: bfloat16 [1024, 3, 1024], P(None, None, 'blk'), may hold values from -0.1875 to 0.1875
- w_out: bfloat16 [1024, 1024], P('blk'), may hold values from -0.5625 to 0.5625
- b_out: bfloat16 [1024], replicated, may hold values from -3 to 3
- gain1: bfloat16 [1024], replicated, may hold values from 0.5 to 1.5
- shift1: bfloat16 [1024], replicated, may hold values from -2 to 2
- w_up: bfloat16 [1024, 4096], P(None, 'blk'), may hold values from -0.1875 to 0.1875
- b_up: bfloat16 [4096], P('blk'), may hold values from -3 to 3
- w_down: bfloat16 [4096, 1024], P('blk'), may hold values from -0.09375 to 0.09375
- b_down: bfloat16 [1024], replicated, may hold values from -3 to 3
- gain2: bfloat16 [1024], replicated, may hold values from 0.5 to 1.5
- shift2: bfloat16 [1024], replicated, may hold values from -2 to 2
- root_cache: bfloat16 [2, 4, 1024, 1024], P(None, None, 'owner', 'blk'), may hold values from -90 to 90
- node_cache: bfloat16 [2, 128, 384, 1024], P(None, 'owner', None, 'blk'), may hold values from -90 to 90
- root_len: int32 [4], replicated, may hold values from 128 to 1024
- node_len: int32 [128], replicated, may hold values from 48 to 384
- node_parent: int32 [128], replicated, may hold values from 0 to 31, as said below
- node_place: int32 [128], replicated, may hold values from 0 to 127, as said below
- req_leaf: int32 [2048], P('owner'), may hold values from 32 to 127, as said below
Outputs:
- result: bfloat16 [2048, 32, 1024], P(('owner', 'blk'))
- new_caches: bfloat16 [2, 2048, 32, 1024], P(None, 'owner', None, 'blk')
Inputs may be any that keep to these rules, and one draw needn't show every extreme that they name: `node_parent`: entries below 32 are branch nodes and name their tenant; each other entry is a leaf and names its branch node; every branch node has exactly three leaves. `node_place`: a permutation of the pool slots; slot s lies on owner s // 2. `req_leaf`: always a leaf; the requests of one owner index lie below different branch nodes.
All inputs are finite; a program needn't handle non-finite values.
Results may differ from a plain program's by a relative error of at most 0.02.
Values may be sent and summed in bfloat16 or wider, within the bound.
No kernel may reach another device: no remote copies, remote signals or barrier semaphores. Data moves between devices by JAX's collectives and lax.ppermute only.
A program may use at most 128 MiB of HBM per device.

v0:
```python
import math
import jax
import jax.numpy as jnp
from jax import lax
from jax.sharding import PartitionSpec as P

HD = 64
norm_eps = 1e-05
masked_score = -1e30


def layer_norm(values, gain, shift):
    center = values - jnp.mean(values, axis=-1, keepdims=True)
    spread = jnp.mean(center * center, axis=-1, keepdims=True)
    return center * lax.rsqrt(spread + norm_eps) * gain.astype(jnp.float32) + shift.astype(
        jnp.float32
    )


def attend_own(queries, key_rows, value_rows, score_scale):
    scores = (
        jnp.einsum("rshe,rnhe->rshn", queries, key_rows, preferred_element_type=jnp.float32)
        * score_scale
    )
    peak = jnp.max(scores, axis=-1)
    weights = jnp.exp(scores - peak[..., None])
    weight_sum = jnp.sum(weights, axis=-1)
    mixed = jnp.einsum(
        "rshn,rnhe->rshe",
        weights.astype(jnp.bfloat16),
        value_rows,
        preferred_element_type=jnp.float32,
    )
    return (mixed / weight_sum[..., None], peak + jnp.log(weight_sum))


def on_device(
    tokens,
    w_qkv,
    w_out,
    b_out,
    gain1,
    shift1,
    w_up,
    b_up,
    w_down,
    b_down,
    gain2,
    shift2,
    root_cache,
    node_cache,
    root_len,
    node_len,
    node_parent,
    node_place,
    req_leaf,
):
    req_dev, suffix, model_width = tokens.shape
    head_cols = w_qkv.shape[2]
    local_heads = head_cols // HD
    own_rows = req_dev * suffix
    owners = lax.axis_size("owner")
    group_size = req_leaf.shape[0]
    score_scale = 1.0 / math.sqrt(HD)
    flat_qkv = w_qkv.reshape(model_width, 3 * head_cols)
    shard_rows = lax.all_gather(tokens, "blk", axis=0, tiled=True)
    row_count = shard_rows.shape[0]
    mixed = jnp.dot(
        shard_rows.reshape(row_count * suffix, model_width),
        flat_qkv,
        preferred_element_type=jnp.float32,
    )
    projected = mixed.astype(jnp.bfloat16).reshape(row_count, suffix, 3 * head_cols)
    queries = projected[:, :, :head_cols].reshape(group_size, suffix, local_heads, HD)
    keys_new = projected[:, :, head_cols : 2 * head_cols]
    values_new = projected[:, :, 2 * head_cols :]
    new_caches = jnp.stack([keys_new, values_new])
    branch = node_parent[req_leaf]
    tenant = node_parent[branch]
    root_limit = root_len[tenant]
    roots_all = lax.all_gather(root_cache, "owner", axis=2, tiled=True)
    root_rows = roots_all.shape[2]
    block_len = math.gcd(root_rows, 256)

    def root_block(block_index, state):
        peak, weight_sum, weighted = state
        offset = block_index * block_len
        key_rows = lax.dynamic_slice_in_dim(roots_all[0], offset, block_len, 1)
        value_rows = lax.dynamic_slice_in_dim(roots_all[1], offset, block_len, 1)
        key_block = jnp.take(key_rows, tenant, axis=0).reshape(
            group_size, block_len, local_heads, HD
        )
        value_block = jnp.take(value_rows, tenant, axis=0).reshape(
            group_size, block_len, local_heads, HD
        )
        positions = offset + jnp.arange(block_len, dtype=jnp.int32)
        in_range = (positions[None, :] < root_limit[:, None])[:, None, None, :]
        scores = (
            jnp.einsum("rshe,rnhe->rshn", queries, key_block, preferred_element_type=jnp.float32)
            * score_scale
        )
        scores = jnp.where(in_range, scores, masked_score)
        new_peak = jnp.maximum(peak, jnp.max(scores, axis=-1))
        weights = jnp.where(in_range, jnp.exp(scores - new_peak[..., None]), 0.0)
        factor = jnp.exp(peak - new_peak)
        weight_sum = weight_sum * factor + jnp.sum(weights, axis=-1)
        weighted = weighted * factor[..., None] + jnp.einsum(
            "rshn,rnhe->rshe",
            weights.astype(jnp.bfloat16),
            value_block,
            preferred_element_type=jnp.float32,
        )
        return (new_peak, weight_sum, weighted)

    start_state = (
        jnp.full((group_size, suffix, local_heads), masked_score, jnp.float32),
        jnp.zeros((group_size, suffix, local_heads), jnp.float32),
        jnp.zeros((group_size, suffix, local_heads, HD), jnp.float32),
    )
    root_peak, root_sum, root_weighted = lax.fori_loop(
        0, root_rows // block_len, root_block, start_state
    )
    root_out = root_weighted / root_sum[..., None]
    root_mass = root_peak + jnp.log(root_sum)
    slot_total = node_place.shape[0]
    slot_count = slot_total // owners
    node_max = node_cache.shape[2]
    slot_ids = jnp.arange(slot_total, dtype=jnp.int32)
    at_branch = slot_ids[:, None] == node_place[branch][None, :]
    at_leaf = slot_ids[:, None] == node_place[req_leaf][None, :]
    route = (at_branch | at_leaf).astype(jnp.bfloat16)
    outgoing = jnp.dot(
        route, queries.reshape(group_size, suffix * head_cols), preferred_element_type=jnp.float32
    )
    outgoing = outgoing.astype(jnp.bfloat16).reshape(owners, slot_count, suffix, head_cols)
    slot_len = jnp.sum(
        jnp.where(slot_ids[:, None] == node_place[None, :], node_len[None, :], 0), axis=1
    )
    my_owner = lax.axis_index("owner")
    local_len = lax.dynamic_slice_in_dim(slot_len, my_owner * slot_count, slot_count)
    cache_keys = node_cache[0].reshape(slot_count, node_max, local_heads, HD)
    cache_values = node_cache[1].reshape(slot_count, node_max, local_heads, HD)
    local_range = jnp.arange(node_max, dtype=jnp.int32)[None, :] < local_len[:, None]
    incoming = lax.all_to_all(outgoing, "owner", split_axis=0, concat_axis=0, tiled=True)
    sources, _, row_count, _ = incoming.shape
    block_width = 8
    blocks = incoming.reshape(
        sources // block_width, block_width, slot_count, row_count, local_heads, HD
    )

    def source_block(block_queries):
        scores = (
            jnp.einsum(
                "bkthe,knhe->bkthn", block_queries, cache_keys, preferred_element_type=jnp.float32
            )
            * score_scale
        )
        keep_rows = local_range[None, :, None, None, :]
        scores = jnp.where(keep_rows, scores, masked_score)
        peak = jnp.max(scores, axis=-1)
        weights = jnp.where(keep_rows, jnp.exp(scores - peak[..., None]), 0.0)
        weight_sum = jnp.sum(weights, axis=-1)
        mixed = jnp.einsum(
            "bkthn,knhe->bkthe",
            weights.astype(jnp.bfloat16),
            cache_values,
            preferred_element_type=jnp.float32,
        )
        mixed = mixed / weight_sum[..., None]
        return (
            mixed.reshape(block_width, slot_count, row_count, head_cols),
            peak + jnp.log(weight_sum),
        )

    mixed, log_mass = lax.map(source_block, blocks)
    mixed = mixed.reshape(sources, slot_count, row_count, head_cols)
    log_mass = log_mass.reshape(sources, slot_count, row_count, local_heads)
    back_out = lax.all_to_all(mixed, "owner", split_axis=0, concat_axis=0, tiled=True)
    back_mass = lax.all_to_all(log_mass, "owner", split_axis=0, concat_axis=0, tiled=True)
    back_flat = back_out.reshape(slot_total, suffix * head_cols)
    mass_flat = back_mass.reshape(slot_total, suffix * local_heads)

    def collect(selected):
        weights_sel = selected.astype(jnp.float32)
        gathered = jnp.einsum("gr,gf->rf", weights_sel, back_flat, precision=lax.Precision.HIGHEST)
        masses = jnp.einsum("gr,gf->rf", weights_sel, mass_flat, precision=lax.Precision.HIGHEST)
        return (
            gathered.reshape(group_size, suffix, local_heads, HD),
            masses.reshape(group_size, suffix, local_heads),
        )

    branch_out, branch_mass = collect(at_branch)
    leaf_out, leaf_mass = collect(at_leaf)
    own_out, own_mass = attend_own(
        queries,
        keys_new.reshape(group_size, suffix, local_heads, HD),
        values_new.reshape(group_size, suffix, local_heads, HD),
        score_scale,
    )
    set_outs = [root_out, branch_out, leaf_out, own_out]
    set_masses = [root_mass, branch_mass, leaf_mass, own_mass]
    highest = jnp.maximum(jnp.maximum(root_mass, branch_mass), jnp.maximum(leaf_mass, own_mass))
    mass_sum = (
        jnp.exp(root_mass - highest)
        + jnp.exp(branch_mass - highest)
        + jnp.exp(leaf_mass - highest)
        + jnp.exp(own_mass - highest)
    )
    total = highest + jnp.log(mass_sum)
    attn = set_outs[0] * jnp.exp(set_masses[0] - total)[..., None]
    for set_index in range(1, 4):
        attn = attn + set_outs[set_index] * jnp.exp(set_masses[set_index] - total)[..., None]
    attn = attn.astype(jnp.bfloat16).reshape(group_size, suffix, head_cols)
    attn_flat = attn.reshape(group_size * suffix, head_cols)
    head_sum = lax.psum_scatter(
        jnp.dot(attn_flat, w_out, preferred_element_type=jnp.float32).astype(jnp.bfloat16),
        "blk",
        scatter_dimension=0,
        tiled=True,
    ).astype(jnp.float32)
    first_norm = layer_norm(
        tokens.reshape(own_rows, model_width).astype(jnp.float32)
        + head_sum
        + b_out.astype(jnp.float32),
        gain1,
        shift1,
    ).astype(jnp.bfloat16)
    inner_act = jnp.dot(
        lax.all_gather(first_norm, "blk", axis=0, tiled=True),
        w_up,
        preferred_element_type=jnp.float32,
    ) + b_up.astype(jnp.float32)
    hidden = jax.nn.gelu(inner_act, approximate=False).astype(jnp.bfloat16)
    down_sum = lax.psum_scatter(
        jnp.dot(hidden, w_down, preferred_element_type=jnp.float32).astype(jnp.bfloat16),
        "blk",
        scatter_dimension=0,
        tiled=True,
    ).astype(jnp.float32)
    result = layer_norm(
        first_norm.astype(jnp.float32) + down_sum + b_down.astype(jnp.float32), gain2, shift2
    ).astype(jnp.bfloat16)
    return (result.reshape(req_dev, suffix, model_width), new_caches)


def solution(mesh):
    in_specs = (
        P(("owner", "blk"), None, None),
        P(None, None, "blk"),
        P("blk", None),
        P(),
        P(),
        P(),
        P(None, "blk"),
        P("blk"),
        P("blk", None),
        P(),
        P(),
        P(),
        P(None, None, "owner", "blk"),
        P(None, "owner", None, "blk"),
        P(),
        P(),
        P(),
        P(),
        P("owner"),
    )
    out_specs = (P(("owner", "blk"), None, None), P(None, "owner", None, "blk"))
    return jax.shard_map(
        on_device, mesh=mesh, in_specs=in_specs, out_specs=out_specs, check_vma=False
    )
```

profile of v0, /device:TPU:2, one launch (start us, length us, event | category | flops | bytes accessed | tf_op | source)
XLA Modules:
  0.0 547.2 jit_solution(3773147124506278843)
XLA Ops:
  13.0 44.8 %all-gather.6.cloned.1.call-done = bf16[32,32,1024]{2,1,0:T(8,128)(2,1)} async-done(((bf16[4,32,1024]{2,1,0:T(8,128)(2,1)}), bf16[32,32,1024]{2,1,0:T(8,128)(2,1)}) %all-gather.6.cloned.1.call-update) | async-done | bytes 2097168 | tf_op jit(solution)/shard_map/all_gather | solution.py:66
  63.4 14.2 %all-to-all-start = ((bf16[64,2,32,128]{3,2,1,0:T(8,128)(2,1)}), bf16[64,2,32,128]{3,2,1,0:T(8,128)(2,1)}, u32[]{:S(2)}, u32[]{:S(2)}) async-start(bf16[64,2,32,128]{3,2,1,0:T(8,128)(2,1)} %bitcast.57), calls=%async_computation | async-start | bytes 2097152 | tf_op jit(solution)/shard_map/all_to_all | solution.py:144
  88.7 18.2 %all-to-all-done = bf16[64,2,32,128]{3,2,1,0:T(8,128)(2,1)} async-done(((bf16[64,2,32,128]{3,2,1,0:T(8,128)(2,1)}), bf16[64,2,32,128]{3,2,1,0:T(8,128)(2,1)}, u32[]{:S(2)}, u32[]{:S(2)}) %all-to-all-start) | async-done | bytes 1048608 | tf_op jit(solution)/shard_map/all_to_all | solution.py:144
  107.0 5.0 reshape.205
  112.0 39.3 %while.31 = (s32[]{:T(128)}, f32[8,8,2,32,128]{4,3,2,1,0:T(8,128)}, f32[8,8,2,32,2]{3,1,0,4,2:T(8,128)}, bf16[8,8,2,32,2,64]{5,4,3,2,1,0:T(2,128)(2,1)}, bf16[2,...) while((s32[]{:T(128)}, f32[8,8,2,32,128]{4,3,2,1,0:T(8,128)}, ...), condition=%wide.region_8.10_spmd.clone, body=%wide.region_5.9_spmd.clone.sunk | while | flops 104267520 | bytes 7389281 | solution.py:175
  153.1 7.8 %all-to-all-start.1 = ((f32[64,1,128]{2,1,0:T(1,128)}), f32[64,1,128]{2,1,0:T(1,128)S(1)}, u32[]{:S(2)}, u32[]{:S(2)}) async-start(f32[64,1,128]{2,1,0:T(1,128)} %reshape.304), calls=%async_computation.1 | async-start | bytes 65536 | tf_op jit(solution)/shard_map/all_to_all | solution.py:179
  163.9 10.5 %all-to-all-done.1 = f32[64,1,128]{2,1,0:T(1,128)S(1)} async-done(((f32[64,1,128]{2,1,0:T(1,128)}), f32[64,1,128]{2,1,0:T(1,128)S(1)}, u32[]{:S(2)}, u32[]{:S(2)}) %all-to-all-start.1) | async-done | bytes 32800 | tf_op jit(solution)/shard_map/all_to_all | solution.py:179
  175.0 6.4 %all-to-all-start.2 = ((f32[64,2,32,128]{3,2,1,0:T(8,128)}), f32[64,2,32,128]{3,2,1,0:T(8,128)}, u32[]{:S(2)}, u32[]{:S(2)}) async-start(f32[64,2,32,128]{3,2,1,0:T(8,128)} %bitcast.197), calls=%async_computation.2 | async-start | bytes 4194304 | tf_op jit(solution)/shard_map/all_to_all | solution.py:178
  181.6 88.1 %all-gather.4.cloned.1.call-done = bf16[2,4,1024,128]{3,2,1,0:T(8,128)(2,1)} async-done(((bf16[2,4,16,128]{3,2,1,0:T(8,128)(2,1)}), bf16[2,4,1024,128]{3,2,1,0:T(8,128)(2,1)}) %all-gather.4.cloned.1.call-update) | async-done | bytes 2097168 | tf_op jit(solution)/shard_map/all_gather | solution.py:81
  269.7 106.4 %while.32 = (s32[]{:T(128)}, f32[32,32,2]{1,2,0:T(2,128)S(1)}, f32[32,32,2]{1,2,0:T(2,128)S(1)}, f32[32,32,2,64]{3,1,2,0:T(8,128)}, s32[32]{0:T(128)S(1)}, /*ind...) while((s32[]{:T(128)}, f32[32,32,2]{1,2,0:T(2,128)S(1)}, ...), condition=%wide.region_3.5_spmd.clone, body=%wide.region_0.4_spmd.clone.sunk | while | flops 143543840 | bytes 50766020 | solution.py:120
  276.5 4.1 broadcast_select_fusion.4
  280.6 4.1 copy.240
  288.1 4.1 copy.241
  292.2 4.0 fusion.189
  303.0 4.1 broadcast_select_fusion.4
  307.1 4.1 copy.240
  314.6 4.1 copy.241
  318.8 4.0 fusion.189
  329.6 4.1 broadcast_select_fusion.4
  333.7 4.1 copy.240
  341.3 4.1 copy.241
  345.4 4.0 fusion.189
  356.3 4.1 broadcast_select_fusion.4
  360.4 4.1 copy.240
  367.9 4.1 copy.241
  372.0 4.0 fusion.189
  387.4 5.2 fusion.43
  392.7 4.0 fusion.46
  399.7 38.1 %reduce-scatter.3.cloned.1.call-done = bf16[128,1024]{1,0:T(8,128)(2,1)} async-done(((bf16[1024,1024]{1,0:T(8,128)(2,1)}), bf16[128,1024]{1,0:T(8,128)(2,1)}) %reduce-scatter.3.cloned.1.call-update) | async-done | bytes 262160 | tf_op jit(solution)/shard_map/reduce_scatter | solution.py:215
  442.1 41.3 %all-gather.8.cloned.1.call-done = bf16[1024,1024]{1,0:T(8,128)(2,1)} async-done(((bf16[128,1024]{1,0:T(8,128)(2,1)}), bf16[1024,1024]{1,0:T(8,128)(2,1)}) %all-gather.8.cloned.1.call-update) | async-done | bytes 2097168 | tf_op jit(solution)/shard_map/all_gather | solution.py:229
  483.4 9.0 %convolution_convert_fusion.1 = bf16[1024,1024]{1,0:T(8,128)(2,1)} fusion(bf16[512,1024]{1,0:T(8,128)(2,1)S(1)} %copy-done, bf16[1024,1024]{1,0:T(8,128)(2,1)} %all-gather.8.cloned.1.call-done, bf16[1024,512]{1,0:T(8,128)(2,1)S(1)} %copy-done.27, f32[512]{0:T(512)S(1)} %convert_element_type.89), kind=kOutput, calls=%fused_computation.81 | convolution fusion | flops 2183135232 | bytes 6293504 | tf_op jit(solution)/shard_map/dot_general | solution.py:235
  494.3 41.7 %reduce-scatter.5.cloned.1.call-done = bf16[128,1024]{1,0:T(8,128)(2,1)} async-done(((bf16[1024,1024]{1,0:T(8,128)(2,1)}), bf16[128,1024]{1,0:T(8,128)(2,1)}) %reduce-scatter.5.cloned.1.call-update) | async-done | bytes 262160 | tf_op jit(solution)/shard_map/reduce_scatter | solution.py:234
  (286 shorter events, 131.3 us)
Async XLA Ops:
  8.0 475.4 %copy-start = (bf16[512,1024]{1,0:T(8,128)(2,1)S(1)}, bf16[512,1024]{1,0:T(8,128)(2,1)}, u32[]{:S(2)}) copy-start(bf16[512,1024]{1,0:T(8,128)(2,1)} %param.33) | copy-start | bytes 3145732
  8.0 2.8 copy-start.1
  8.0 3.5 copy-start.2
  8.0 49.7 %all-gather.6.cloned.1.call-start = ((), (), s32[]{:S(2)}) async-start(), calls=%async_computation.6 | async-start | bytes 2359296 | tf_op jit(solution)/shard_map/all_gather | solution.py:66
  62.2 16.7 %copy-start.12 = (bf16[2,2,384,128]{3,2,1,0:T(8,128)(2,1)S(1)}, bf16[2,2,384,128]{3,2,1,0:T(8,128)(2,1)}, u32[]{:S(2)}) copy-start(bf16[2,2,384,128]{3,2,1,0:T(8,128)(2,1)} %param.38) | copy-start | bytes 1179652
  63.4 16.6 %copy-start.28 = (s32[128]{0:T(128)S(1)}, s32[128]{0:T(128)}, u32[]{:S(2)}) copy-start(s32[128]{0:T(128)} %param.40) | copy-start | bytes 1540
  63.4 16.7 %copy-start.17 = (s32[4]{0:T(128)S(1)}, s32[4]{0:T(128)}, u32[]{:S(2)}) copy-start(s32[4]{0:T(128)} %param.39) | copy-start | bytes 52
  63.4 43.6 %all-to-all-start = ((bf16[64,2,32,128]{3,2,1,0:T(8,128)(2,1)}), bf16[64,2,32,128]{3,2,1,0:T(8,128)(2,1)}, u32[]{:S(2)}, u32[]{:S(2)}) async-start(bf16[64,2,32,128]{3,2,1,0:T(8,128)(2,1)} %bitcast.57), calls=%async_computation | async-start | bytes 2097152 | tf_op jit(solution)/shard_map/all_to_all | solution.py:144
  77.6 192.1 %all-gather.4.cloned.1.call-start = ((), (), s32[]{:S(2)}) async-start(), calls=%async_computation.5 | async-start | bytes 2129920 | tf_op jit(solution)/shard_map/all_gather | solution.py:81
  83.7 5.1 copy-start.5
  88.7 23.2 %copy-start.14 = (bf16[1,2,384,128]{2,3,1,0:T(8,128)(2,1)S(1)}, bf16[1,2,384,128]{2,3,1,0:T(8,128)(2,1)}, u32[]{:S(2)}) copy-start(bf16[1,2,384,128]{2,3,1,0:T(8,128)(2,1)} %copy.135) | copy-start | bytes 589828
  153.1 21.3 %all-to-all-start.1 = ((f32[64,1,128]{2,1,0:T(1,128)}), f32[64,1,128]{2,1,0:T(1,128)S(1)}, u32[]{:S(2)}, u32[]{:S(2)}) async-start(f32[64,1,128]{2,1,0:T(1,128)} %reshape.304), calls=%async_computation.1 | async-start | bytes 65536 | tf_op jit(solution)/shard_map/all_to_all | solution.py:179
  175.0 207.3 %all-to-all-start.2 = ((f32[64,2,32,128]{3,2,1,0:T(8,128)}), f32[64,2,32,128]{3,2,1,0:T(8,128)}, u32[]{:S(2)}, u32[]{:S(2)}) async-start(f32[64,2,32,128]{3,2,1,0:T(8,128)} %bitcast.197), calls=%async_computation.2 | async-start | bytes 4194304 | tf_op jit(solution)/shard_map/all_to_all | solution.py:178
  181.4 256.5 %reduce-scatter.3.cloned.1.call-start = ((), (), s32[]{:S(2)}) async-start(), calls=%async_computation.7 | async-start | bytes 2359296 | tf_op jit(solution)/shard_map/reduce_scatter | solution.py:215
  273.6 2.8 copy-start.3
  292.2 4.0 copy-start.25
  300.2 2.8 copy-start.3
  318.8 4.1 copy-start.25
  326.8 2.8 copy-start.3
  345.4 4.1 copy-start.25
  353.4 2.8 copy-start.3
  372.0 4.1 copy-start.25
  387.4 5.3 copy-start.7
  387.4 5.3 copy-start.9
  387.4 5.3 copy-start.16
  392.6 4.9 copy-start.13
  397.5 40.3 %copy-start.6 = (bf16[4,32,1024]{2,1,0:T(8,128)(2,1)S(1)}, bf16[4,32,1024]{2,1,0:T(8,128)(2,1)}, u32[]{:S(2)}) copy-start(bf16[4,32,1024]{2,1,0:T(8,128)(2,1)} %param.25) | copy-start | bytes 786436
  399.6 42.5 %copy-start.26 = (bf16[512]{0:T(512)(128)(2,1)S(1)}, bf16[512]{0:T(512)(128)(2,1)}, u32[]{:S(2)}) copy-start(bf16[512]{0:T(512)(128)(2,1)} %param.32) | copy-start | bytes 3076
  399.6 83.8 %copy-start.27 = (bf16[1024,512]{1,0:T(8,128)(2,1)S(1)}, bf16[1024,512]{1,0:T(8,128)(2,1)}, u32[]{:S(2)}) copy-start(bf16[1024,512]{1,0:T(8,128)(2,1)} %param.31) | copy-start | bytes 3145732
  399.6 83.8 %all-gather.8.cloned.1.call-start = ((), (), s32[]{:S(2)}) async-start(), calls=%async_computation.8 | async-start | bytes 2359296 | tf_op jit(solution)/shard_map/all_gather | solution.py:229
  442.0 94.0 %reduce-scatter.5.cloned.1.call-start = ((), (), s32[]{:S(2)}) async-start(), calls=%async_computation.9 | async-start | bytes 2359296 | tf_op jit(solution)/shard_map/reduce_scatter | solution.py:234
  492.4 43.6 %copy-start.4 = (bf16[128,1024]{1,0:T(8,128)(2,1)S(1)}, bf16[128,1024]{1,0:T(8,128)(2,1)}, u32[]{:S(2)}) copy-start(bf16[128,1024]{1,0:T(8,128)(2,1)} %add_convert_fusion.1) | copy-start | bytes 786436
  (14 other events, 19.8 us)
Sparse Core Ops, SparseCore 0:
  10.9 46.7 all-gather.5
  399.7 38.0 reduce-scatter.2
  442.1 41.2 all-gather.7
  492.6 43.3 reduce-scatter.4
Sparse Core Ops, SparseCore 1:
  82.4 187.2 all-gather.3
where the time goes:
time: 549 us; the launch traced here: 547 us
  waiting for transfers between devices  284 us (52%)
  local copies, waits for them, and re-layouts  110 us (20%)
  matrix products  61.6 us (11%)
  other arithmetic  46.7 us (9%)
  starting transfers between devices  28.8 us (5%)
  between operations  15.7 us (3%)
    all_gather x1, waiting for transfers between devices, on_device(): roots_all = lax.all_gather(root_cache, 'owner', axis=2, tiled=True)  88.1 us
    all_gather x1, waiting for transfers between devices, on_device(): shard_rows = lax.all_gather(tokens, 'blk', axis=0, tiled=True)  44.8 us
    reduce_scatter x1, waiting for transfers between devices, on_device(): lax.psum_scatter(jnp.dot(hidden, w_down, preferred_element_type=jnp.float...  41.7 us
    all_gather x1, waiting for transfers between devices, on_device(): lax.all_gather(first_norm, 'blk', axis=0, tiled=True)  41.3 us
    reduce_scatter x1, waiting for transfers between devices, on_device(): lax.psum_scatter(jnp.dot(attn_flat, w_out, preferred_element_type=jnp.flo...  38.1 us
    all_to_all x1, waiting for transfers between devices, on_device(): lax.all_to_all(outgoing, 'owner', split_axis=0, concat_axis=0, tiled=True)  18.2 us
    select_n x4, local copies, waits for them, and re-layouts, root_block(): jnp.take(value_rows, tenant, axis=0)  16.4 us
    select_n x4, local copies, waits for them, and re-layouts, root_block(): jnp.take(key_rows, tenant, axis=0)  16.4 us
  transfers between devices with their start and end apart: 8, of which 7 were waited for; matrix products, arithmetic and copies ran while one was open for 32% of the time, Pallas kernels for 0%

commit v1 on v0

--- a/solution.py
+++ b/solution.py
@@ -226,7 +226,9 @@
         shift1,
     ).astype(jnp.bfloat16)
     inner_act = jnp.dot(
-        lax.all_gather(first_norm, "blk", axis=0, tiled=True),
+        jnp.concatenate(
+            lax.all_to_all(jnp.stack([first_norm] * lax.axis_size("blk")), "blk", 0, 0), axis=0
+        ),
         w_up,
         preferred_element_type=jnp.float32,
     ) + b_up.astype(jnp.float32)

time: 549 us -> 561 us (1.022)
  waiting for transfers between devices: 284 us -> 291 us
    all_to_all x0 -> x1, waiting for transfers between devices: none -> 48.9 us  [on_device(): lax.all_to_all(jnp.stack([first_norm] * lax.axis_size('blk')), 'blk', 0, 0)]
    all_gather x1 -> x0, waiting for transfers between devices: 41.3 us -> none  [on_device(): lax.all_gather(first_norm, 'blk', axis=0, tiled=True)]
where the time goes in v1:
time: 561 us; the launch traced here: 559 us
  waiting for transfers between devices  291 us (52%)
  local copies, waits for them, and re-layouts  111 us (20%)
  matrix products  61.6 us (11%)
  other arithmetic  46.2 us (8%)
  starting transfers between devices  32.5 us (6%)
  between operations  15.7 us (3%)
    all_gather x1, waiting for transfers between devices, on_device(): roots_all = lax.all_gather(root_cache, 'owner', axis=2, tiled=True)  88.1 us
    all_to_all x1, waiting for transfers between devices, on_device(): lax.all_to_all(jnp.stack([first_norm] * lax.axis_size('blk')), 'blk', 0, 0)  48.9 us
    all_gather x1, waiting for transfers between devices, on_device(): shard_rows = lax.all_gather(tokens, 'blk', axis=0, tiled=True)  44.8 us
    reduce_scatter x1, waiting for transfers between devices, on_device(): lax.psum_scatter(jnp.dot(hidden, w_down, preferred_element_type=jnp.float...  41.5 us
    reduce_scatter x1, waiting for transfers between devices, on_device(): lax.psum_scatter(jnp.dot(attn_flat, w_out, preferred_element_type=jnp.flo...  38 us
    all_to_all x1, waiting for transfers between devices, on_device(): lax.all_to_all(outgoing, 'owner', split_axis=0, concat_axis=0, tiled=True)  18.4 us
    select_n x4, local copies, waits for them, and re-layouts, root_block(): jnp.take(value_rows, tenant, axis=0)  16.3 us
    select_n x4, other arithmetic, root_block(): jnp.take(value_rows, tenant, axis=0)  16.3 us
  transfers between devices with their start and end apart: 8, of which 7 were waited for; matrix products, arithmetic and copies ran while one was open for 32% of the time, Pallas kernels for 0%

profile of v1, /device:TPU:2, one launch (start us, length us, event | category | flops | bytes accessed | tf_op | source)
XLA Modules:
  0.0 559.1 jit_solution(5901508390413226402)
XLA Ops:
  13.0 44.8 %all-gather.5.cloned.1.call-done = bf16[32,32,1024]{2,1,0:T(8,128)(2,1)} async-done(((bf16[4,32,1024]{2,1,0:T(8,128)(2,1)}), bf16[32,32,1024]{2,1,0:T(8,128)(2,1)}) %all-gather.5.cloned.1.call-update) | async-done | bytes 2097168 | tf_op jit(solution)/shard_map/all_gather | solution.py:66
  63.4 14.2 %all-to-all-start = ((bf16[64,2,32,128]{3,2,1,0:T(8,128)(2,1)}), bf16[64,2,32,128]{3,2,1,0:T(8,128)(2,1)}, u32[]{:S(2)}, u32[]{:S(2)}) async-start(bf16[64,2,32,128]{3,2,1,0:T(8,128)(2,1)} %bitcast.58), calls=%async_computation | async-start | bytes 2097152 | tf_op jit(solution)/shard_map/all_to_all | solution.py:144
  88.6 18.4 %all-to-all-done = bf16[64,2,32,128]{3,2,1,0:T(8,128)(2,1)} async-done(((bf16[64,2,32,128]{3,2,1,0:T(8,128)(2,1)}), bf16[64,2,32,128]{3,2,1,0:T(8,128)(2,1)}, u32[]{:S(2)}, u32[]{:S(2)}) %all-to-all-start) | async-done | bytes 1048608 | tf_op jit(solution)/shard_map/all_to_all | solution.py:144
  107.0 5.0 reshape.210
  111.9 39.3 %while.31 = (s32[]{:T(128)}, f32[8,8,2,32,128]{4,3,2,1,0:T(8,128)}, f32[8,8,2,32,2]{3,1,0,4,2:T(8,128)}, bf16[8,8,2,32,2,64]{5,4,3,2,1,0:T(2,128)(2,1)}, bf16[2,...) while((s32[]{:T(128)}, f32[8,8,2,32,128]{4,3,2,1,0:T(8,128)}, ...), condition=%wide.region_8.10_spmd.clone, body=%wide.region_5.9_spmd.clone.sunk | while | flops 104267520 | bytes 7389281 | solution.py:175
  153.0 7.9 %all-to-all-start.1 = ((f32[64,1,128]{2,1,0:T(1,128)}), f32[64,1,128]{2,1,0:T(1,128)S(1)}, u32[]{:S(2)}, u32[]{:S(2)}) async-start(f32[64,1,128]{2,1,0:T(1,128)} %reshape.310), calls=%async_computation.1 | async-start | bytes 65536 | tf_op jit(solution)/shard_map/all_to_all | solution.py:179
  163.8 10.5 %all-to-all-done.1 = f32[64,1,128]{2,1,0:T(1,128)S(1)} async-done(((f32[64,1,128]{2,1,0:T(1,128)}), f32[64,1,128]{2,1,0:T(1,128)S(1)}, u32[]{:S(2)}, u32[]{:S(2)}) %all-to-all-start.1) | async-done | bytes 32800 | tf_op jit(solution)/shard_map/all_to_all | solution.py:179
  174.9 6.4 %all-to-all-start.2 = ((f32[64,2,32,128]{3,2,1,0:T(8,128)}), f32[64,2,32,128]{3,2,1,0:T(8,128)}, u32[]{:S(2)}, u32[]{:S(2)}) async-start(f32[64,2,32,128]{3,2,1,0:T(8,128)} %bitcast.198), calls=%async_computation.2 | async-start | bytes 4194304 | tf_op jit(solution)/shard_map/all_to_all | solution.py:178
  181.5 88.1 %all-gather.3.cloned.1.call-done = bf16[2,4,1024,128]{3,2,1,0:T(8,128)(2,1)} async-done(((bf16[2,4,16,128]{3,2,1,0:T(8,128)(2,1)}), bf16[2,4,1024,128]{3,2,1,0:T(8,128)(2,1)}) %all-gather.3.cloned.1.call-update) | async-done | bytes 2097168 | tf_op jit(solution)/shard_map/all_gather | solution.py:81
  269.6 106.3 %while.32 = (s32[]{:T(128)}, f32[32,32,2]{1,2,0:T(2,128)S(1)}, f32[32,32,2]{1,2,0:T(2,128)S(1)}, f32[32,32,2,64]{3,1,2,0:T(8,128)}, s32[32]{0:T(128)S(1)}, /*ind...) while((s32[]{:T(128)}, f32[32,32,2]{1,2,0:T(2,128)S(1)}, ...), condition=%wide.region_3.5_spmd.clone, body=%wide.region_0.4_spmd.clone.sunk | while | flops 143543840 | bytes 50766020 | solution.py:120
  276.5 4.1 broadcast_select_fusion.4
  280.6 4.1 copy.240
  288.1 4.1 copy.241
  292.2 3.9 fusion.189
  303.0 4.1 broadcast_select_fusion.4
  307.1 4.1 copy.240
  314.6 4.1 copy.241
  318.7 4.0 fusion.189
  329.6 4.1 broadcast_select_fusion.4
  333.7 4.1 copy.240
  341.2 4.1 copy.241
  345.3 4.0 fusion.189
  356.2 4.1 broadcast_select_fusion.4
  360.3 4.1 copy.240
  367.8 4.1 copy.241
  371.9 4.0 fusion.189
  387.4 5.2 fusion.43
  392.7 4.0 fusion.46
  399.7 38.0 %reduce-scatter.3.cloned.1.call-done = bf16[128,1024]{1,0:T(8,128)(2,1)} async-done(((bf16[1024,1024]{1,0:T(8,128)(2,1)}), bf16[128,1024]{1,0:T(8,128)(2,1)}) %reduce-scatter.3.cloned.1.call-update) | async-done | bytes 262160 | tf_op jit(solution)/shard_map/reduce_scatter | solution.py:215
  446.5 48.9 %all-to-all-done.3 = bf16[8,128,1024]{2,1,0:T(8,128)(2,1)S(1)} async-done(((bf16[8,128,1024]{2,1,0:T(8,128)(2,1)}), bf16[8,128,1024]{2,1,0:T(8,128)(2,1)S(1)}, u32[]{:S(2)}, u32[]{:S(2)}) %all-to-all-start.3) | async-done | bytes 2097184 | tf_op jit(solution)/shard_map/all_to_all | solution.py:230
  495.4 9.0 %convolution_convert_fusion.1 = bf16[1024,1024]{1,0:T(8,128)(2,1)} fusion(bf16[512,1024]{1,0:T(8,128)(2,1)S(1)} %copy-done, bf16[1024,1024]{1,0:T(8,128)(2,1)S(1)} %bitcast.201, bf16[1024,512]{1,0:T(8,128)(2,1)} %param.31, f32[512]{0:T(512)S(1)} %convert_element_type.89), kind=kOutput, calls=%fused_computation.81 | convolution fusion | flops 2183135232 | bytes 6293504 | tf_op jit(solution)/shard_map/dot_general | solution.py:237
  506.4 41.5 %reduce-scatter.5.cloned.1.call-done = bf16[128,1024]{1,0:T(8,128)(2,1)} async-done(((bf16[1024,1024]{1,0:T(8,128)(2,1)}), bf16[128,1024]{1,0:T(8,128)(2,1)}) %reduce-scatter.5.cloned.1.call-update) | async-done | bytes 262160 | tf_op jit(solution)/shard_map/reduce_scatter | solution.py:236
  (282 shorter events, 136.0 us)
Async XLA Ops:
  8.0 487.4 %copy-start = (bf16[512,1024]{1,0:T(8,128)(2,1)S(1)}, bf16[512,1024]{1,0:T(8,128)(2,1)}, u32[]{:S(2)}) copy-start(bf16[512,1024]{1,0:T(8,128)(2,1)} %param.33) | copy-start | bytes 3145732
  8.0 2.8 copy-start.1
  8.0 3.5 copy-start.2
  8.0 49.7 %all-gather.5.cloned.1.call-start = ((), (), s32[]{:S(2)}) async-start(), calls=%async_computation.7 | async-start | bytes 2359296 | tf_op jit(solution)/shard_map/all_gather | solution.py:66
  62.2 16.7 %copy-start.11 = (bf16[2,2,384,128]{3,2,1,0:T(8,128)(2,1)S(1)}, bf16[2,2,384,128]{3,2,1,0:T(8,128)(2,1)}, u32[]{:S(2)}) copy-start(bf16[2,2,384,128]{3,2,1,0:T(8,128)(2,1)} %param.38) | copy-start | bytes 1179652
  63.4 16.6 %copy-start.26 = (s32[128]{0:T(128)S(1)}, s32[128]{0:T(128)}, u32[]{:S(2)}) copy-start(s32[128]{0:T(128)} %param.40) | copy-start | bytes 1540
  63.4 16.8 %copy-start.16 = (s32[4]{0:T(128)S(1)}, s32[4]{0:T(128)}, u32[]{:S(2)}) copy-start(s32[4]{0:T(128)} %param.39) | copy-start | bytes 52
  63.4 43.6 %all-to-all-start = ((bf16[64,2,32,128]{3,2,1,0:T(8,128)(2,1)}), bf16[64,2,32,128]{3,2,1,0:T(8,128)(2,1)}, u32[]{:S(2)}, u32[]{:S(2)}) async-start(bf16[64,2,32,128]{3,2,1,0:T(8,128)(2,1)} %bitcast.58), calls=%async_computation | async-start | bytes 2097152 | tf_op jit(solution)/shard_map/all_to_all | solution.py:144
  77.6 192.1 %all-gather.3.cloned.1.call-start = ((), (), s32[]{:S(2)}) async-start(), calls=%async_computation.6 | async-start | bytes 2129920 | tf_op jit(solution)/shard_map/all_gather | solution.py:81
  83.5 5.1 copy-start.4
  88.6 23.4 %copy-start.13 = (bf16[1,2,384,128]{2,3,1,0:T(8,128)(2,1)S(1)}, bf16[1,2,384,128]{2,3,1,0:T(8,128)(2,1)}, u32[]{:S(2)}) copy-start(bf16[1,2,384,128]{2,3,1,0:T(8,128)(2,1)} %copy.135) | copy-start | bytes 589828
  153.0 21.3 %all-to-all-start.1 = ((f32[64,1,128]{2,1,0:T(1,128)}), f32[64,1,128]{2,1,0:T(1,128)S(1)}, u32[]{:S(2)}, u32[]{:S(2)}) async-start(f32[64,1,128]{2,1,0:T(1,128)} %reshape.310), calls=%async_computation.1 | async-start | bytes 65536 | tf_op jit(solution)/shard_map/all_to_all | solution.py:179
  174.9 207.4 %all-to-all-start.2 = ((f32[64,2,32,128]{3,2,1,0:T(8,128)}), f32[64,2,32,128]{3,2,1,0:T(8,128)}, u32[]{:S(2)}, u32[]{:S(2)}) async-start(f32[64,2,32,128]{3,2,1,0:T(8,128)} %bitcast.198), calls=%async_computation.2 | async-start | bytes 4194304 | tf_op jit(solution)/shard_map/all_to_all | solution.py:178
  181.3 256.4 %reduce-scatter.3.cloned.1.call-start = ((), (), s32[]{:S(2)}) async-start(), calls=%async_computation.8 | async-start | bytes 2359296 | tf_op jit(solution)/shard_map/reduce_scatter | solution.py:215
  273.6 2.9 copy-start.3
  292.2 4.0 copy-start.24
  300.1 2.9 copy-start.3
  318.7 4.0 copy-start.24
  326.7 2.9 copy-start.3
  345.3 4.0 copy-start.24
  353.3 2.9 copy-start.3
  371.9 4.0 copy-start.24
  387.4 5.3 copy-start.6
  387.4 5.3 copy-start.8
  387.4 5.3 copy-start.15
  392.7 4.9 copy-start.12
  397.6 2.1 copy-start.18
  397.6 2.1 copy-start.19
  397.6 40.1 %copy-start.5 = (bf16[4,32,1024]{2,1,0:T(8,128)(2,1)S(1)}, bf16[4,32,1024]{2,1,0:T(8,128)(2,1)}, u32[]{:S(2)}) copy-start(bf16[4,32,1024]{2,1,0:T(8,128)(2,1)} %param.25) | copy-start | bytes 786436
  442.7 3.8 copy-start.25
  442.7 52.7 %all-to-all-start.3 = ((bf16[8,128,1024]{2,1,0:T(8,128)(2,1)}), bf16[8,128,1024]{2,1,0:T(8,128)(2,1)S(1)}, u32[]{:S(2)}, u32[]{:S(2)}) async-start(bf16[8,128,1024]{2,1,0:T(8,128)(2,1)} %stack.8), calls=%async_computation.4 | async-start | bytes 4194304 | tf_op jit(solution)/shard_map/all_to_all | solution.py:230
  446.4 101.4 %reduce-scatter.5.cloned.1.call-start = ((), (), s32[]{:S(2)}) async-start(), calls=%async_computation.9 | async-start | bytes 2359296 | tf_op jit(solution)/shard_map/reduce_scatter | solution.py:236
  (12 other events, 15.4 us)
Sparse Core Ops, SparseCore 0:
  10.9 46.7 all-gather.4
  399.8 37.8 reduce-scatter.2
  504.6 43.2 reduce-scatter.4
Sparse Core Ops, SparseCore 1:
  82.4 187.2 all-gather.2
